TPU v7x, 32 devices: a whole 2x2x4 slice. The times are simulated.
32 devices in a mesh: grp: 2 (over core), seq: 8 (over z, y), tp: 2 (over x).
Axes of the slice: x: 2, y: 2, z: 4, core: 2. Of those that a mesh axis runs over, the one named last changes fastest.
Arguments:
- prompt_states: bfloat16 [2, 16384, 4096], P(None, ('grp', 'seq'), 'tp'), may hold values from -40 to 40
- q_weight: bfloat16 [4096, 16, 128], P(None, 'tp'), may hold values from -0.09375 to 0.09375
- kv_weight: bfloat16 [4096, 2, 4, 128], P(None, None, 'tp'), may hold values from -0.09375 to 0.09375
- lengths: int32 [2], replicated, may hold values from 4096 to 16384, as said below
- sink_positions: int32 [2, 4], replicated, may hold values from 0 to 2047
Outputs:
- attended: bfloat16 [2, 16384, 2048], P(None, ('grp', 'seq'), 'tp')
- kv_cache: bfloat16 [2, 4, 2, 8, 1024, 256], P(None, ('tp', 'grp'), None, 'seq')
Inputs may be any that keep to these rules, and one draw needn't show every extreme that they name: `lengths`: at least one request has length 16384.
All inputs are finite; a program needn't handle non-finite values.
Results may differ from a plain program's by a relative error of at most 0.0065.
Values may be sent and summed in bfloat16 or wider, within the bound.
No kernel may reach another device: no remote copies, remote signals or barrier semaphores. Data moves between devices by JAX's collectives and lax.ppermute only.
A program may use at most 512 MiB of HBM per device.

v0:
```python
import math
import jax
import jax.numpy as jnp
from jax import lax
from jax.sharding import PartitionSpec as P

WINDOW = 4096
ROPE_BASE = 10000.0
NEG_FILL = -1e30


def shifted(block, axis, distance):
    devices = range(lax.axis_size(axis))
    route = [(i - distance, i) for i in devices if i - distance in devices]
    return lax.ppermute(block, axis, route)


def rotate(vectors, positions):
    head_dim = vectors.shape[-1]
    half_dim = head_dim // 2
    ladder = jnp.arange(half_dim, dtype=jnp.float32) * (2.0 / head_dim)
    inv_freq = jnp.exp(-math.log(ROPE_BASE) * ladder)
    angles = positions.astype(jnp.float32)[:, None] * inv_freq[None, :]
    cosine = jnp.cos(angles)[None, :, None, :]
    sine_part = jnp.sin(angles)[None, :, None, :]
    lead_half = vectors[..., :half_dim]
    tail_half = vectors[..., half_dim:]
    return jnp.concatenate(
        [lead_half * cosine - tail_half * sine_part, tail_half * cosine + lead_half * sine_part],
        axis=-1,
    )


def window_mask(key_pos, query_pos, lengths, sink_positions):
    sink_flag = jnp.any(key_pos[:, :, None] == sink_positions[:, None, :], axis=2)
    distance = query_pos[None, :, None] - key_pos[:, None, :]
    in_window = distance < WINDOW
    return (
        (distance >= 0)
        & (key_pos[:, None, :] >= 0)
        & (key_pos[:, None, :] < lengths[:, None, None])
        & (in_window | sink_flag[:, None, :])
    )


def attend(carried, in_block, visible, queries, inv_root):
    running, sums_now, weighted = carried
    scores = (
        jnp.einsum(
            "rqhgd,rkhd->rhgqk", queries, in_block[:, :, 0], preferred_element_type=jnp.float32
        )
        * inv_root
    )
    masked = visible[:, None, None]
    scores = jnp.where(masked, scores, NEG_FILL)
    new_max = jnp.maximum(running, jnp.max(scores, axis=-1))
    weights = jnp.where(masked, jnp.exp(scores - new_max[..., None]), 0.0)
    factor = jnp.exp(running - new_max)
    sums_now = sums_now * factor + jnp.sum(weights, axis=-1)
    weight_rows = weights.astype(jnp.bfloat16)
    weighted = weighted * factor[..., None] + jnp.einsum(
        "rhgqk,rkhd->rhgqd", weight_rows, in_block[:, :, 1], preferred_element_type=jnp.float32
    )
    return (new_max, sums_now, weighted)


def per_device(prompt_states, q_weight, kv_weight, lengths, sink_positions):
    num_reqs, slab_len, half_width = prompt_states.shape
    model_width, local_heads, head_dim = q_weight.shape
    kv_local = kv_weight.shape[2]
    share_count = local_heads // kv_local
    token_count = num_reqs * slab_len
    q_matrix = q_weight.reshape(model_width, local_heads * head_dim)
    kv_matrix = kv_weight.reshape(model_width, 2 * kv_local * head_dim)
    shard_part = lax.all_gather(prompt_states, "tp", axis=2, tiled=True)
    columns = shard_part.shape[2]
    flattened = shard_part.reshape(token_count, columns)
    query_raw = jnp.dot(flattened, q_matrix, preferred_element_type=jnp.float32)
    kv_raw = jnp.dot(flattened, kv_matrix, preferred_element_type=jnp.float32)
    device_index = lax.axis_index(("grp", "seq"))
    span_slabs = (WINDOW - 1) // slab_len + 1
    anchor = device_index * slab_len
    positions = anchor + jnp.arange(slab_len, dtype=jnp.int32)
    queries = rotate(
        query_raw.reshape(num_reqs, slab_len, local_heads, head_dim), positions
    ).astype(jnp.bfloat16)
    queries = queries.reshape(num_reqs, slab_len, kv_local, share_count, head_dim)
    kv_raw = kv_raw.reshape(num_reqs, slab_len, 2, kv_local, head_dim)
    key_rows = rotate(kv_raw[:, :, 0], positions).astype(jnp.bfloat16)
    values = kv_raw[:, :, 1].astype(jnp.bfloat16)
    own_rows = jnp.stack([key_rows, values], axis=2)
    inv_root = 1.0 / math.sqrt(head_dim)

    def fold_block(carried, in_block, key_line):
        key_pos = jnp.broadcast_to(key_line[None, :], (num_reqs, key_line.shape[0]))
        return attend(
            carried,
            in_block,
            window_mask(key_pos, positions, lengths, sink_positions),
            queries,
            inv_root,
        )

    carried = (
        jnp.full((num_reqs, kv_local, share_count, slab_len), NEG_FILL, jnp.float32),
        jnp.zeros((num_reqs, kv_local, share_count, slab_len), jnp.float32),
        jnp.zeros((num_reqs, kv_local, share_count, slab_len, head_dim), jnp.float32),
    )
    carried = fold_block(carried, own_rows, positions)
    held_rows = own_rows
    held_pos = positions
    stride = 1
    while stride < span_slabs:
        incoming = shifted(held_rows, ("grp", "seq"), stride)
        incoming_pos = held_pos - stride * slab_len
        carried = fold_block(carried, incoming, incoming_pos)
        if stride * 2 < span_slabs:
            held_rows = jnp.concatenate([incoming, held_rows], axis=1)
            held_pos = jnp.concatenate([incoming_pos, held_pos])
        stride = stride * 2
    farthest = shifted(own_rows, ("grp", "seq"), span_slabs)
    carried = fold_block(carried, farthest, positions - span_slabs * slab_len)
    sink_hits = (sink_positions[:, :, None] == positions[None, None, :]).astype(jnp.bfloat16)
    sink_terms = jnp.einsum(
        "rks,rsxhd->rkxhd", sink_hits, own_rows, preferred_element_type=jnp.float32
    )
    sink_block = lax.psum(sink_terms, ("grp", "seq")).astype(jnp.bfloat16)
    mark_count = sink_positions.shape[1]
    earlier = jnp.arange(mark_count)[None, :] < jnp.arange(mark_count)[:, None]
    repeated = jnp.any(
        (sink_positions[:, :, None] == sink_positions[:, None, :]) & earlier[None], axis=2
    )
    uncovered = sink_positions < (device_index - span_slabs) * slab_len
    sink_usable = ~repeated & uncovered & (sink_positions < lengths[:, None])
    sink_visible = sink_usable[:, None, :] & (
        sink_positions[:, None, :] <= positions[None, :, None]
    )
    carried = attend(carried, sink_block, sink_visible, queries, inv_root)
    running, sums_now, weighted = carried
    mixed = weighted / sums_now[..., None]
    mixed = jnp.transpose(mixed, (0, 3, 1, 2, 4)).reshape(
        num_reqs, slab_len, local_heads * head_dim
    )
    live_rows = positions[None, :] < lengths[:, None]
    attended = jnp.where(live_rows[:, :, None], mixed, 0.0).astype(jnp.bfloat16)
    cache_rows = jnp.concatenate([key_rows, values], axis=-1)
    cache_rows = jnp.where(live_rows[:, :, None, None], cache_rows, jnp.zeros_like(cache_rows))
    pieces = jnp.transpose(cache_rows, (0, 2, 1, 3)).reshape(
        num_reqs, kv_local, 1, 1, slab_len, 2 * head_dim
    )
    kv_cache = lax.all_to_all(pieces, "grp", split_axis=1, concat_axis=2, tiled=True)
    return (attended, kv_cache)


def solution(mesh):
    placed = (
        P(None, ("grp", "seq"), "tp"),
        P(None, "tp", None),
        P(None, None, "tp", None),
        P(),
        P(),
    )
    return jax.shard_map(
        per_device,
        mesh=mesh,
        in_specs=placed,
        out_specs=(P(None, ("grp", "seq"), "tp"), P(None, ("tp", "grp"), None, "seq", None, None)),
        check_vma=False,
    )
```

profile of v0, /device:TPU:0, one launch (start us, length us, event | category | flops | bytes accessed | tf_op | source)
XLA Modules:
  0.0 840.8 jit_solution(16857945234379509448)
XLA Ops:
  7.2 0.0 all-gather.2.cloned.1.call-start
  7.2 0.7 all-gather.2.cloned.1.call-update
  7.9 7.2 reshape.486
  15.1 6.7 copy.42
  21.8 11.3 %copy.89 = bf16[512,8,8,128]{3,1,2,0:T(8,128)(2,1)} copy(bf16[512,8,8,128]{3,2,1,0:T(8,128)(2,1)} %bitcast.331) | data formatting | bytes 16777216
  33.1 11.6 %copy.44 = bf16[1024,4096]{1,0:T(8,128)(2,1)} copy(bf16[1024,4096]{0,1:T(8,128)(2,1)} %bitcast.323) | data formatting | bytes 16777216 | tf_op jit(solution)/shard_map/dot_general | solution.py:78
  44.8 0.2 and_reduce_fusion
  45.0 0.1 compare_reduce_fusion
  45.1 0.1 compare_and_fusion.1
  45.2 0.2 compare_reduce_fusion.1
  45.4 0.1 broadcast_compare_fusion.4
  45.5 1.8 multiply_cosine_fusion
  47.2 0.1 broadcast_compare_fusion
  47.3 6.6 fusion.30
  54.0 9.3 %fusion.39 = (pred[2,1024,1024]{1,2,0:T(8,128)(4,1)S(1)}, pred[2,1024,1024]{1,2,0:T(8,128)(4,1)}, pred[2,1024,1024]{1,2,0:T(8,128)(4,1)}) fusion(s32[1024]{0:T(1024)S(1)} %iota_add_fusion, pred[1024]{0:T(1024)(128)(4,1)S(1)} %get-tuple-element.47, pred[2,1024]{1,0:T(4,128)(4,1)S(1)} %get-tuple-element.10, pred[2,1024]{1,0:T(4,128)(4,1)S(1)} %get-tuple-element.32, ...), kind=kLoop, calls=%fused_computation.58 | loop fusion | flops 44040192 | bytes 6319104 | tf_op jit(solution)/shard_map/and | solution.py:39
  63.2 147.9 %all-gather.2.cloned.1.call-done = bf16[2,1024,4096]{2,1,0:T(8,128)(2,1)} async-done(((bf16[2,1024,2048]{2,1,0:T(8,128)(2,1)}), bf16[2,1024,4096]{2,1,0:T(8,128)(2,1)}) %all-gather.2.cloned.1.call-update) | async-done | bytes 16777232 | tf_op jit(solution)/shard_map/all_gather | solution.py:75
  211.1 13.1 %fusion.26 = f32[2,1024,2,2,128]{1,4,3,2,0:T(8,128)S(1)} fusion(bf16[2,2,128,4096,1]{3,2,1,0,4:T(8,128)(2,1)} %bitcast.335, bf16[2,1024,4096]{2,1,0:T(8,128)(2,1)} %all-gather.2.cloned.1.call-done), kind=kOutput, calls=%fused_computation.32 | convolution fusion | flops 8589934592 | bytes 25165824 | tf_op jit(solution)/shard_map/dot_general | solution.py:79
  224.3 0.0 slice-start
  224.3 0.1 slice_bitcast_fusion.4
  224.4 0.2 slice.96
  224.6 0.0 slice-start.1
  224.6 0.4 subtract_convert_fusion.1
  225.0 1.9 copy-done.2
  226.9 1.6 pad_maximum_fusion.1
  228.5 5.0 collective-permute-start
  233.5 4.8 collective-permute-start.2
  238.3 1.2 slice_bitcast_fusion.17
  239.5 21.0 %fusion.24 = f32[2,1024,8,128]{1,3,2,0:T(8,128)S(1)} fusion(bf16[8,128,4096,1]{2,1,0,3:T(8,128)(2,1)S(1)} %bitcast.334, bf16[2,1024,4096]{2,1,0:T(8,128)(2,1)} %all-gather.2.cloned.1.call-done), kind=kOutput, calls=%fused_computation.30 | convolution fusion | flops 17179869184 | bytes 33554432 | tf_op jit(solution)/shard_map/dot_general | solution.py:78
  260.6 3.5 subtract_convert_fusion
  264.1 4.8 copy.45
  268.9 4.7 copy.46
  273.6 1.8 fusion.52
  275.4 1.5 copy.58
  276.9 5.0 all-to-all-start
  281.9 4.6 pad_maximum_fusion
  286.6 0.0 copy-start
  286.6 2.0 copy-done
  288.6 23.9 %fusion.6 = (f32[2,2,4,1024]{3,2,1,0:T(4,128)S(1)}, f32[2,2,1024,1024,4]{3,2,4,1,0:T(8,128)}) fusion(pred[2,1024,1024]{1,2,0:T(8,128)(4,1)S(1)} %get-tuple-element.29, bf16[2,1024,2,4,128]{4,1,3,2,0:T(8,128)(2,1)S(1)} %pad_maximum_fusion, bf16[2,1024,2,64]{1,3,2,0:T(8,128)(2,1)S(1)} %get-tuple-element.22, bf16[2,1024,2,64]{1,3,2,0:T(8,128)(2,1)S(1)} %get-tuple-element.21), kind=kOutput, calls=%fused_computation.13 | convolution fusion | flops 4347379712 | bytes 74514432 | tf_op jit(solution)/shard_map/rqhgd,rkhd->rhgqk/dot_general | solution.py:49
  312.5 0.0 all-to-all-done
  312.5 3.9 copy.59
  316.5 2.2 fusion.76
  318.7 99.8 %psum.7 = bf16[2,4,2,2,128]{4,1,3,2,0:T(4,128)(2,1)S(1)} all-reduce(f32[2,4,2,2,128]{4,1,3,2,0:T(4,128)S(1)} %fusion.76), channel_id=1, replica_groups=mesh['grp'=2,'seq'=8,'tp'=2] {'grp','seq'}, use_global_device_ids=true, to_apply=%region_9.10 | all-reduce | flops 4096 | bytes 24576 | tf_op jit(solution)/shard_map/psum | solution.py:127
  418.5 4.3 fusion.103
  422.7 3.6 maximum_maximum_fusion
  426.3 3.7 collective-permute-start.1
  430.0 25.6 %fusion.7 = (f32[2,2,4,1024]{3,2,1,0:T(4,128)S(1)}, f32[2,2,1024,1024,4]{3,2,4,1,0:T(8,128)}) fusion(pred[2,1024,1024]{1,2,0:T(8,128)(4,1)} %get-tuple-element.31, bf16[2,1024,2,4,128]{4,1,3,2,0:T(8,128)(2,1)S(1)} %copy-done.1, bf16[2,1024,2,2,128]{1,4,3,2,0:T(8,128)(2,1)} %collective-permute-done), kind=kOutput, calls=%fused_computation.14 | convolution fusion | flops 4345282560 | bytes 74514432 | tf_op jit(solution)/shard_map/rqhgd,rkhd->rhgqk/dot_general | solution.py:49
  455.6 0.0 collective-permute-done.2
  455.6 25.0 %fusion.8 = (f32[2,2,4,1024]{3,2,1,0:T(4,128)S(1)}, f32[2,2,1024,1024,4]{3,2,4,1,0:T(8,128)}) fusion(pred[2,1024,1024]{1,2,0:T(8,128)(4,1)S(1)} %copy-done.3, bf16[2,1024,2,4,128]{4,1,3,2,0:T(8,128)(2,1)S(1)} %copy-done.1, bf16[2,1024,2,2,128]{1,4,3,2,0:T(8,128)(2,1)} %collective-permute-done.2), kind=kOutput, calls=%fused_computation.15 | convolution fusion | flops 4345282560 | bytes 74514432 | tf_op jit(solution)/shard_map/rqhgd,rkhd->rhgqk/dot_general | solution.py:49
  480.6 38.3 %collective-permute-done.1 = bf16[2,2048,2,2,128]{1,4,3,2,0:T(8,128)(2,1)} collective-permute-done((bf16[2,2048,2,2,128]{1,4,3,2,0:T(8,128)(2,1)}, bf16[2,2048,2,2,128]{1,4,3,2,0:T(8,128)(2,1)}, u32[]{:S(2)}, u32[]{:S(2)}) %collective-permute-start.1) | collective-permute-done | bytes 4194336 | tf_op jit(solution)/shard_map/ppermute | solution.py:15
  518.9 48.3 %fusion = (f32[2,2,4,1024]{3,2,1,0:T(4,128)S(1)}, f32[2,2,2048,1024,4]{3,2,4,1,0:T(8,128)}) fusion(pred[2,1024,2048]{1,2,0:T(8,128)(4,1)} %fusion.30, bf16[2,1024,2,4,128]{4,1,3,2,0:T(8,128)(2,1)} %copy-done, bf16[2,2048,2,2,128]{1,4,3,2,0:T(8,128)(2,1)} %collective-permute-done.1), kind=kOutput, calls=%fused_computation.2 | convolution fusion | flops 8690581504 | bytes 144769024 | tf_op jit(solution)/shard_map/rqhgd,rkhd->rhgqk/dot_general | solution.py:49
  567.2 0.1 fusion.101
  567.3 21.7 %fusion.9 = f32[2,2,4,1024]{3,2,1,0:T(4,128)S(1)} fusion(f32[2,2,1024,1024,4]{3,2,4,1,0:T(8,128)} %get-tuple-element.44, f32[2,2,4,1024]{3,2,1,0:T(4,128)S(1)} %get-tuple-element.25, pred[2,1024,1024]{1,2,0:T(8,128)(4,1)S(1)} %get-tuple-element.29), kind=kLoop, calls=%fused_computation.16 | loop fusion | flops 83869696 | bytes 69337088 | tf_op jit(solution)/shard_map/reduce_sum | solution.py:59
  589.0 29.2 %fusion.19 = f32[2,2,4,1024,128]{3,4,2,1,0:T(8,128)} fusion(f32[2,2,1024,1024,4]{3,2,4,1,0:T(8,128)} %get-tuple-element.44, f32[2,2,4,1024]{3,2,1,0:T(4,128)S(1)} %get-tuple-element.25, pred[2,1024,1024]{1,2,0:T(8,128)(4,1)S(1)} %get-tuple-element.29, f32[2,1024,2,2,128]{1,4,3,2,0:T(8,128)} %copy-done.6), kind=kOutput, calls=%fused_computation.24 | convolution fusion | flops 4378853376 | bytes 78708736 | tf_op jit(solution)/shard_map/rhgqk,rkhd->rhgqd/dot_general | solution.py:61
  618.2 0.3 fusion.61
  618.5 4.6 fusion.63
  623.1 21.7 %fusion.11 = f32[2,2,4,1024]{3,2,1,0:T(4,128)S(1)} fusion(f32[2,2,1024,1024,4]{3,2,4,1,0:T(8,128)} %get-tuple-element.42, f32[2,2,4,1024]{3,2,1,0:T(4,128)S(1)} %get-tuple-element.18, pred[2,1024,1024]{1,2,0:T(8,128)(4,1)S(1)} %copy-done.5), kind=kLoop, calls=%fused_computation.18 | loop fusion | flops 83869696 | bytes 69337088 | tf_op jit(solution)/shard_map/reduce_sum | solution.py:59
  644.8 42.6 %fusion.1 = f32[2,2,4,1024]{3,2,1,0:T(4,128)S(1)} fusion(f32[2,2,2048,1024,4]{3,2,4,1,0:T(8,128)} %get-tuple-element.40, f32[2,2,4,1024]{3,2,1,0:T(4,128)S(1)} %get-tuple-element.17, pred[2,1024,2048]{1,2,0:T(8,128)(4,1)} %fusion.30), kind=kLoop, calls=%fused_computation.3 | loop fusion | flops 167755776 | bytes 138543104 | tf_op jit(solution)/shard_map/reduce_sum | solution.py:59
  687.4 21.7 %fusion.13 = f32[2,2,4,1024]{3,2,1,0:T(4,128)S(1)} fusion(f32[2,2,1024,1024,4]{3,2,4,1,0:T(8,128)} %get-tuple-element.38, f32[2,2,4,1024]{3,2,1,0:T(4,128)S(1)} %get-tuple-element.16, pred[2,1024,1024]{1,2,0:T(8,128)(4,1)S(1)} %copy-done.4), kind=kLoop, calls=%fused_computation.20 | loop fusion | flops 83869696 | bytes 69337088 | tf_op jit(solution)/shard_map/reduce_sum | solution.py:59
  709.1 0.1 bitcast_add_fusion.5
  709.3 29.0 %fusion.17 = f32[2,2,4,1024,128]{3,4,2,1,0:T(8,128)} fusion(f32[2,2,1024,1024,4]{3,2,4,1,0:T(8,128)} %get-tuple-element.42, f32[2,2,4,1024]{3,2,1,0:T(4,128)S(1)} %get-tuple-element.18, pred[2,1024,1024]{1,2,0:T(8,128)(4,1)} %get-tuple-element.31, bf16[2,1024,2,2,128]{1,4,3,2,0:T(8,128)(2,1)} %collective-permute-done), kind=kOutput, calls=%fused_computation.23 | convolution fusion | flops 4378853376 | bytes 78708736 | tf_op jit(solution)/shard_map/rhgqk,rkhd->rhgqd/dot_general | solution.py:61
  738.2 50.0 %fusion.3 = f32[2,2,4,1024,128]{3,4,2,1,0:T(8,128)} fusion(f32[2,2,2048,1024,4]{3,2,4,1,0:T(8,128)} %get-tuple-element.40, f32[2,2,4,1024]{3,2,1,0:T(4,128)S(1)} %get-tuple-element.17, pred[2,1024,2048]{1,2,0:T(8,128)(4,1)} %fusion.30, bf16[2,2048,2,2,128]{1,4,3,2,0:T(8,128)(2,1)} %collective-permute-done.1), kind=kOutput, calls=%fused_computation.11 | convolution fusion | flops 8757706752 | bytes 148963328 | tf_op jit(solution)/shard_map/rhgqk,rkhd->rhgqd/dot_general | solution.py:61
  788.2 35.3 %fusion.32 = bf16[2,1024,2,4,128]{1,4,3,2,0:T(8,128)(2,1)} fusion(f32[2,2,4,1024,128]{3,4,2,1,0:T(8,128)} %fusion.63, f32[2,2,4,1024,128]{3,4,2,1,0:T(8,128)} %fusion.3, f32[2,2,4,1024,128]{3,4,2,1,0:T(8,128)} %fusion.17, f32[2,2,4,1024,128]{3,4,2,1,0:T(8,128)} %fusion.19, f32[2,1024,2,4]{1,3,2,0:T(4,128)S(1)} %get-tuple-element.11, ...), kind=kOutput, calls=%fused_computation.46 | convolution fusion | flops 4401922048 | bytes 108462080 | tf_op jit(solution)/shard_map/rhgqk,rkhd->rhgqd/dot_general | solution.py:61
  823.5 6.2 copy.57
  829.7 4.0 select_convert_fusion
  (44 shorter events, 0.1 us)
Async XLA Ops:
  7.2 204.0 %all-gather.2.cloned.1.call-start = ((), (), s32[]{:S(2)}) async-start(), calls=%async_computation.1 | async-start | bytes 25165824 | tf_op jit(solution)/shard_map/all_gather | solution.py:75
  33.1 11.7 %copy-start.13 = (s32[2,4]{1,0:T(2,128)S(1)}, s32[2,4]{1,0:T(2,128)}, u32[]{:S(2)}) copy-start(s32[2,4]{1,0:T(2,128)} %param.9) | copy-start | bytes 100
  33.1 12.0 %copy-start.16 = (s32[2]{0:T(128)S(1)}, s32[2]{0:T(128)}, u32[]{:S(2)}) copy-start(s32[2]{0:T(128)} %param.8) | copy-start | bytes 28
  45.4 373.1 %copy-start.9 = (pred[2,1024,4]{1,2,0:T(4,128)(4,1)}, pred[2,1024,4]{1,2,0:T(4,128)(4,1)S(1)}, u32[]{:S(2)}) copy-start(pred[2,1024,4]{1,2,0:T(4,128)(4,1)S(1)} %get-tuple-element.26) | copy-start | bytes 24580
  45.5 228.2 %copy-start.11 = (pred[2,1024]{1,0:T(4,128)(4,1)}, pred[2,1024]{1,0:T(4,128)(4,1)S(1)}, u32[]{:S(2)}) copy-start(pred[2,1024]{1,0:T(4,128)(4,1)S(1)} %get-tuple-element.32) | copy-start | bytes 6148
  211.1 13.5 %copy-start.7 = (f32[1024,64]{0,1:T(8,128)S(1)}, f32[1024,64]{0,1:T(8,128)}, u32[]{:S(2)}) copy-start(f32[1024,64]{0,1:T(8,128)} %get-tuple-element.28) | copy-start | bytes 786436
  224.3 15.2 %copy-start.6 = (f32[2,1024,2,2,128]{1,4,3,2,0:T(8,128)}, f32[2,1024,2,2,128]{1,4,3,2,0:T(8,128)S(1)}, u32[]{:S(2)}) copy-start(f32[2,1024,2,2,128]{1,4,3,2,0:T(8,128)S(1)} %fusion.26) | copy-start | bytes 12582916
  224.3 15.2 %slice-start = ((s8[8388608]{0:T(1024)(128)(4,1)}), s8[4194304]{0:T(1024)(128)(4,1)S(1)}, s32[]{:S(2)}) async-start(s8[8388608]{0:T(1024)(128)(4,1)} %bitcast.332), calls=%async_computation.2 | async-start | bytes 8388608
  224.6 2.3 copy-start.2
  224.6 14.9 %slice-start.1 = ((s8[8388608]{0:T(1024)(128)(4,1)}), s8[4194304]{0:T(1024)(128)(4,1)S(1)}, s32[]{:S(2)}) async-start(s8[8388608]{0:T(1024)(128)(4,1)} %bitcast.332), calls=%async_computation.3 | async-start | bytes 8388608
  228.5 194.2 %collective-permute-start = (bf16[2,1024,2,2,128]{1,4,3,2,0:T(8,128)(2,1)}, bf16[2,1024,2,2,128]{1,4,3,2,0:T(8,128)(2,1)}, u32[]{:S(2)}, u32[]{:S(2)}) collective-permute-start(bf16[2,1024,2,2,128]{1,4,3,2,0:T(8,128)(2,1)} %pad_maximum_fusion.1), channel_id=1, source_target_pairs={{0,2},{2,4},{4,6},{6,8},{8,10},{10,12},{12,14},{14,16},{16,18},{18... | collective-permute-start | bytes 6291464 | tf_op jit(solution)/shard_map/ppermute | solution.py:15
  233.5 222.1 %collective-permute-start.2 = (bf16[2,1024,2,2,128]{1,4,3,2,0:T(8,128)(2,1)}, bf16[2,1024,2,2,128]{1,4,3,2,0:T(8,128)(2,1)}, u32[]{:S(2)}, u32[]{:S(2)}) collective-permute-start(bf16[2,1024,2,2,128]{1,4,3,2,0:T(8,128)(2,1)} %pad_maximum_fusion.1), channel_id=1, source_target_pairs={{0,8},{2,10},{4,12},{6,14},{8,16},{10,18},{12,20},{14,22},{16,24},... | collective-permute-start | bytes 6291464 | tf_op jit(solution)/shard_map/ppermute | solution.py:15
  276.9 35.6 %all-to-all-start = ((bf16[2,2,1,1,1024,256]{4,5,0,3,2,1:T(8,128)(2,1)}), bf16[2,2,1,1,1024,256]{4,5,0,3,2,1:T(8,128)(2,1)}, u32[]{:S(2)}, u32[]{:S(2)}) async-start(bf16[2,2,1,1,1024,256]{4,5,0,3,2,1:T(8,128)(2,1)} %copy.58), calls=%async_computation | async-start | bytes 4194304 | tf_op jit(solution)/shard_map/all_to_all | solution.py:151
  286.6 2.0 copy-start
  418.5 37.1 %copy-start.14 = (bf16[2,4,2,2,128]{4,1,3,2,0:T(4,128)(2,1)}, bf16[2,4,2,2,128]{4,1,3,2,0:T(4,128)(2,1)S(1)}, u32[]{:S(2)}) copy-start(bf16[2,4,2,2,128]{4,1,3,2,0:T(4,128)(2,1)S(1)} %psum.7) | copy-start | bytes 24580
  418.5 11.6 %copy-start.1 = (bf16[2,1024,2,4,128]{4,1,3,2,0:T(8,128)(2,1)S(1)}, bf16[2,1024,2,4,128]{4,1,3,2,0:T(8,128)(2,1)}, u32[]{:S(2)}) copy-start(bf16[2,1024,2,4,128]{4,1,3,2,0:T(8,128)(2,1)} %copy-done) | copy-start | bytes 12582916
  426.3 92.6 %collective-permute-start.1 = (bf16[2,2048,2,2,128]{1,4,3,2,0:T(8,128)(2,1)}, bf16[2,2048,2,2,128]{1,4,3,2,0:T(8,128)(2,1)}, u32[]{:S(2)}, u32[]{:S(2)}) collective-permute-start(bf16[2,2048,2,2,128]{1,4,3,2,0:T(8,128)(2,1)} %maximum_maximum_fusion), channel_id=1, source_target_pairs={{0,4},{2,6},{4,8},{6,10},{8,12},{10,14},{12,16},{14,18},{16,20},{1... | collective-permute-start | bytes 12582920 | tf_op jit(solution)/shard_map/ppermute | solution.py:15
  430.0 25.6 %copy-start.3 = (pred[2,1024,1024]{1,2,0:T(8,128)(4,1)S(1)}, pred[2,1024,1024]{1,2,0:T(8,128)(4,1)}, u32[]{:S(2)}) copy-start(pred[2,1024,1024]{1,2,0:T(8,128)(4,1)} %get-tuple-element.30) | copy-start | bytes 6291460
  589.0 29.3 %copy-start.8 = (f32[2,2,4,1024,4]{3,4,2,1,0:T(4,128)S(1)}, f32[2,2,4,1024,4]{3,4,2,1,0:T(4,128)}, u32[]{:S(2)}) copy-start(f32[2,2,4,1024,4]{3,4,2,1,0:T(4,128)} %get-tuple-element.36) | copy-start | bytes 786436
  589.0 29.3 %copy-start.10 = (pred[2,1024,4]{1,2,0:T(4,128)(4,1)S(1)}, pred[2,1024,4]{1,2,0:T(4,128)(4,1)}, u32[]{:S(2)}) copy-start(pred[2,1024,4]{1,2,0:T(4,128)(4,1)} %copy-done.9) | copy-start | bytes 24580
  589.0 29.5 %copy-start.15 = (bf16[2,4,2,2,128]{4,1,3,2,0:T(4,128)(2,1)S(1)}, bf16[2,4,2,2,128]{4,1,3,2,0:T(4,128)(2,1)}, u32[]{:S(2)}) copy-start(bf16[2,4,2,2,128]{4,1,3,2,0:T(4,128)(2,1)} %copy-done.14) | copy-start | bytes 24580
  618.2 4.9 copy-start.5
  644.8 42.7 %copy-start.4 = (pred[2,1024,1024]{1,2,0:T(8,128)(4,1)S(1)}, pred[2,1024,1024]{1,2,0:T(8,128)(4,1)}, u32[]{:S(2)}) copy-start(pred[2,1024,1024]{1,2,0:T(8,128)(4,1)} %get-tuple-element.30) | copy-start | bytes 6291460
  823.5 6.2 copy-start.12
Sparse Core Ops, SparseCore 0:
  9.5 201.5 all-gather.1
where the time goes:
time: 848 us; the launch traced here: 841 us
  matrix products  311 us (37%)
  waiting for transfers between devices  187 us (22%)
  other arithmetic  146 us (17%)
  blocking collectives  99.8 us (12%)
  local copies, waits for them, and re-layouts  63.4 us (7%)
  starting transfers between devices  18.5 us (2%)
  between operations  14.6 us (2%)
    dot_general x5, matrix products, attend(): jnp.einsum('rhgqk,rkhd->rhgqd', weight_rows, in_block[:, :, 1], preferred...  148 us
    all_gather x1, waiting for transfers between devices, per_device(): shard_part = lax.all_gather(prompt_states, 'tp', axis=2, tiled=True)  148 us
    dot_general x5, matrix products, attend(): jnp.einsum('rqhgd,rkhd->rhgqk', queries, in_block[:, :, 0], preferred_ele...  127 us
    reduce_sum x5, other arithmetic, attend(): sums_now = sums_now * factor + jnp.sum(weights, axis=-1)  108 us
    psum x1, blocking collectives, per_device(): sink_block = lax.psum(sink_terms, ('grp', 'seq')).astype(jnp.bfloat16)  99.8 us
    ppermute x3, waiting for transfers between devices, shifted(): return lax.ppermute(block, axis, route)  38.3 us
    dot_general x1, matrix products, per_device(): query_raw = jnp.dot(flattened, q_matrix, preferred_element_type=jnp.float32)  21 us
    unnamed x40, local copies, waits for them, and re-layouts  19.3 us
  transfers between devices with their start and end apart: 5, of which 2 were waited for; matrix products, arithmetic and copies ran while one was open for 22% of the time, Pallas kernels for 0%

commit v1 on v0

--- a/solution.py
+++ b/solution.py
@@ -7,6 +7,11 @@
 WINDOW = 4096
 ROPE_BASE = 10000.0
 NEG_FILL = -1e30
+
+
+def gather_and_add(x, axis):
+    parts = lax.all_gather(x, axis)
+    return jnp.sum(parts, axis=0)
 
 
 def shifted(block, axis, distance):
@@ -124,7 +129,7 @@
     sink_terms = jnp.einsum(
         "rks,rsxhd->rkxhd", sink_hits, own_rows, preferred_element_type=jnp.float32
     )
-    sink_block = lax.psum(sink_terms, ("grp", "seq")).astype(jnp.bfloat16)
+    sink_block = gather_and_add(sink_terms, ("grp", "seq")).astype(jnp.bfloat16)
     mark_count = sink_positions.shape[1]
     earlier = jnp.arange(mark_count)[None, :] < jnp.arange(mark_count)[:, None]
     repeated = jnp.any(

time: 848 us -> 821 us (0.968)
  blocking collectives: 99.8 us -> 72.6 us
    psum x1 -> x0, blocking collectives: 99.8 us -> none  [per_device(): sink_block = lax.psum(sink_terms, ('grp', 'seq')).astype(jnp.bfloat16)]
    all_gather x0 -> x1, blocking collectives: none -> 72.6 us  [gather_and_add(): parts = lax.all_gather(x, axis)]
  transfers between devices with their start and end apart: 5 -> 5, of which waited for: 2 -> 2; matrix products, arithmetic and copies ran while one was open for 22% -> 23% of each run, Pallas kernels for 0% -> 0%
where the time goes in v1:
time: 821 us; the launch traced here: 814 us
  matrix products  311 us (38%)
  waiting for transfers between devices  186 us (23%)
  other arithmetic  146 us (18%)
  blocking collectives  72.6 us (9%)
  local copies, waits for them, and re-layouts  63.4 us (8%)
  starting transfers between devices  19.3 us (2%)
  between operations  14.6 us (2%)
    dot_general x5, matrix products, attend(): jnp.einsum('rhgqk,rkhd->rhgqd', weight_rows, in_block[:, :, 1], preferred...  148 us
    all_gather x1, waiting for transfers between devices, per_device(): shard_part = lax.all_gather(prompt_states, 'tp', axis=2, tiled=True)  148 us
    dot_general x5, matrix products, attend(): jnp.einsum('rqhgd,rkhd->rhgqk', queries, in_block[:, :, 0], preferred_ele...  127 us
    reduce_sum x5, other arithmetic, attend(): sums_now = sums_now * factor + jnp.sum(weights, axis=-1)  108 us
    all_gather x1, blocking collectives, gather_and_add(): parts = lax.all_gather(x, axis)  72.6 us
    ppermute x3, waiting for transfers between devices, shifted(): return lax.ppermute(block, axis, route)  37.3 us
    dot_general x1, matrix products, per_device(): query_raw = jnp.dot(flattened, q_matrix, preferred_element_type=jnp.float32)  21 us
    unnamed x40, local copies, waits for them, and re-layouts  19.3 us
  transfers between devices with their start and end apart: 5, of which 2 were waited for; matrix products, arithmetic and copies ran while one was open for 23% of the time, Pallas kernels for 0%

profile of v1, /device:TPU:0, one launch (start us, length us, event | category | flops | bytes accessed | tf_op | source)
XLA Modules:
  0.0 813.6 jit_solution(16741182815726496434)
XLA Ops:
  7.2 0.0 all-gather.3.cloned.1.call-start
  7.2 0.7 all-gather.3.cloned.1.call-update
  7.9 7.2 reshape.486
  15.1 6.7 copy.43
  21.8 11.3 %copy.99 = bf16[512,8,8,128]{3,1,2,0:T(8,128)(2,1)} copy(bf16[512,8,8,128]{3,2,1,0:T(8,128)(2,1)} %bitcast.332) | data formatting | bytes 16777216
  33.1 11.6 %copy.45 = bf16[1024,4096]{1,0:T(8,128)(2,1)} copy(bf16[1024,4096]{0,1:T(8,128)(2,1)} %bitcast.324) | data formatting | bytes 16777216 | tf_op jit(solution)/shard_map/dot_general | solution.py:83
  44.8 0.2 and_reduce_fusion
  45.0 0.1 compare_reduce_fusion
  45.1 0.1 compare_and_fusion.1
  45.2 0.2 compare_reduce_fusion.1
  45.4 0.1 broadcast_compare_fusion.4
  45.5 1.8 multiply_cosine_fusion
  47.2 0.1 broadcast_compare_fusion
  47.3 6.6 fusion.30
  54.0 9.3 %fusion.39 = (pred[2,1024,1024]{1,2,0:T(8,128)(4,1)S(1)}, pred[2,1024,1024]{1,2,0:T(8,128)(4,1)}, pred[2,1024,1024]{1,2,0:T(8,128)(4,1)}) fusion(s32[1024]{0:T(1024)S(1)} %iota_add_fusion, pred[1024]{0:T(1024)(128)(4,1)S(1)} %get-tuple-element.47, pred[2,1024]{1,0:T(4,128)(4,1)S(1)} %get-tuple-element.10, pred[2,1024]{1,0:T(4,128)(4,1)S(1)} %get-tuple-element.32, ...), kind=kLoop, calls=%fused_computation.58 | loop fusion | flops 44040192 | bytes 6319104 | tf_op jit(solution)/shard_map/and | solution.py:44
  63.2 147.9 %all-gather.3.cloned.1.call-done = bf16[2,1024,4096]{2,1,0:T(8,128)(2,1)} async-done(((bf16[2,1024,2048]{2,1,0:T(8,128)(2,1)}), bf16[2,1024,4096]{2,1,0:T(8,128)(2,1)}) %all-gather.3.cloned.1.call-update) | async-done | bytes 16777232 | tf_op jit(solution)/shard_map/all_gather | solution.py:80
  211.1 13.1 %fusion.26 = f32[2,1024,2,2,128]{1,4,3,2,0:T(8,128)S(1)} fusion(bf16[2,2,128,4096,1]{3,2,1,0,4:T(8,128)(2,1)} %bitcast.336, bf16[2,1024,4096]{2,1,0:T(8,128)(2,1)} %all-gather.3.cloned.1.call-done), kind=kOutput, calls=%fused_computation.32 | convolution fusion | flops 8589934592 | bytes 25165824 | tf_op jit(solution)/shard_map/dot_general | solution.py:84
  224.3 0.0 slice-start
  224.3 0.1 slice_bitcast_fusion.4
  224.4 0.2 slice.96
  224.6 0.0 slice-start.1
  224.6 0.4 subtract_convert_fusion.1
  225.0 1.9 copy-done.2
  226.9 1.6 pad_maximum_fusion.1
  228.5 5.0 collective-permute-start
  233.5 4.8 collective-permute-start.2
  238.3 1.2 slice_bitcast_fusion.17
  239.5 21.0 %fusion.24 = f32[2,1024,8,128]{1,3,2,0:T(8,128)S(1)} fusion(bf16[8,128,4096,1]{2,1,0,3:T(8,128)(2,1)S(1)} %bitcast.335, bf16[2,1024,4096]{2,1,0:T(8,128)(2,1)} %all-gather.3.cloned.1.call-done), kind=kOutput, calls=%fused_computation.30 | convolution fusion | flops 17179869184 | bytes 33554432 | tf_op jit(solution)/shard_map/dot_general | solution.py:83
  260.6 3.5 subtract_convert_fusion
  264.1 4.8 copy.46
  268.9 4.7 copy.47
  273.6 1.8 fusion.52
  275.4 1.5 copy.60
  276.9 5.0 all-to-all-start
  281.9 4.6 pad_maximum_fusion
  286.6 0.0 copy-start
  286.6 2.0 copy-done
  288.6 23.9 %fusion.6 = (f32[2,2,4,1024]{3,2,1,0:T(4,128)S(1)}, f32[2,2,1024,1024,4]{3,2,4,1,0:T(8,128)}) fusion(pred[2,1024,1024]{1,2,0:T(8,128)(4,1)S(1)} %get-tuple-element.29, bf16[2,1024,2,4,128]{4,1,3,2,0:T(8,128)(2,1)S(1)} %pad_maximum_fusion, bf16[2,1024,2,64]{1,3,2,0:T(8,128)(2,1)S(1)} %get-tuple-element.22, bf16[2,1024,2,64]{1,3,2,0:T(8,128)(2,1)S(1)} %get-tuple-element.21), kind=kOutput, calls=%fused_computation.13 | convolution fusion | flops 4347379712 | bytes 74514432 | tf_op jit(solution)/shard_map/rqhgd,rkhd->rhgqk/dot_general | solution.py:54
  312.5 3.9 copy.61
  316.5 2.2 fusion.76
  318.7 72.6 %all-gather = f32[32,4,2,2,128]{4,1,3,2,0:T(4,128)S(1)} all-gather(f32[2,4,2,2,128]{4,1,3,2,0:T(4,128)S(1)} %fusion.76), channel_id=2, replica_groups=mesh['grp'=2,'seq'=8,'tp'=2] {'grp','seq'}, dimensions={0}, use_global_device_ids=true | all-gather | bytes 278528 | tf_op jit(solution)/shard_map/all_gather | solution.py:13
  391.3 0.1 reduce_sum.64
  391.4 0.0 copy-start.1
  391.4 4.3 fusion.103
  395.7 3.6 maximum_maximum_fusion
  399.2 4.5 collective-permute-start.1
  403.8 25.6 %fusion.7 = (f32[2,2,4,1024]{3,2,1,0:T(4,128)S(1)}, f32[2,2,1024,1024,4]{3,2,4,1,0:T(8,128)}) fusion(pred[2,1024,1024]{1,2,0:T(8,128)(4,1)} %get-tuple-element.31, bf16[2,1024,2,4,128]{4,1,3,2,0:T(8,128)(2,1)S(1)} %copy-done.1, bf16[2,1024,2,2,128]{1,4,3,2,0:T(8,128)(2,1)} %collective-permute-done), kind=kOutput, calls=%fused_computation.14 | convolution fusion | flops 4345282560 | bytes 74514432 | tf_op jit(solution)/shard_map/rqhgd,rkhd->rhgqk/dot_general | solution.py:54
  429.4 25.0 %fusion.8 = (f32[2,2,4,1024]{3,2,1,0:T(4,128)S(1)}, f32[2,2,1024,1024,4]{3,2,4,1,0:T(8,128)}) fusion(pred[2,1024,1024]{1,2,0:T(8,128)(4,1)S(1)} %copy-done.3, bf16[2,1024,2,4,128]{4,1,3,2,0:T(8,128)(2,1)S(1)} %copy-done.1, bf16[2,1024,2,2,128]{1,4,3,2,0:T(8,128)(2,1)} %collective-permute-done.2), kind=kOutput, calls=%fused_computation.15 | convolution fusion | flops 4345282560 | bytes 74514432 | tf_op jit(solution)/shard_map/rqhgd,rkhd->rhgqk/dot_general | solution.py:54
  454.4 37.3 %collective-permute-done.1 = bf16[2,2048,2,2,128]{1,4,3,2,0:T(8,128)(2,1)} collective-permute-done((bf16[2,2048,2,2,128]{1,4,3,2,0:T(8,128)(2,1)}, bf16[2,2048,2,2,128]{1,4,3,2,0:T(8,128)(2,1)}, u32[]{:S(2)}, u32[]{:S(2)}) %collective-permute-start.1) | collective-permute-done | bytes 4194336 | tf_op jit(solution)/shard_map/ppermute | solution.py:20
  491.7 48.3 %fusion = (f32[2,2,4,1024]{3,2,1,0:T(4,128)S(1)}, f32[2,2,2048,1024,4]{3,2,4,1,0:T(8,128)}) fusion(pred[2,1024,2048]{1,2,0:T(8,128)(4,1)} %fusion.30, bf16[2,1024,2,4,128]{4,1,3,2,0:T(8,128)(2,1)} %copy-done, bf16[2,2048,2,2,128]{1,4,3,2,0:T(8,128)(2,1)} %collective-permute-done.1), kind=kOutput, calls=%fused_computation.2 | convolution fusion | flops 8690581504 | bytes 144769024 | tf_op jit(solution)/shard_map/rqhgd,rkhd->rhgqk/dot_general | solution.py:54
  540.0 0.1 fusion.101
  540.0 21.7 %fusion.9 = f32[2,2,4,1024]{3,2,1,0:T(4,128)S(1)} fusion(f32[2,2,1024,1024,4]{3,2,4,1,0:T(8,128)} %get-tuple-element.44, f32[2,2,4,1024]{3,2,1,0:T(4,128)S(1)} %get-tuple-element.25, pred[2,1024,1024]{1,2,0:T(8,128)(4,1)S(1)} %get-tuple-element.29), kind=kLoop, calls=%fused_computation.16 | loop fusion | flops 83869696 | bytes 69337088 | tf_op jit(solution)/shard_map/reduce_sum | solution.py:64
  561.8 29.2 %fusion.19 = f32[2,2,4,1024,128]{3,4,2,1,0:T(8,128)} fusion(f32[2,2,1024,1024,4]{3,2,4,1,0:T(8,128)} %get-tuple-element.44, f32[2,2,4,1024]{3,2,1,0:T(4,128)S(1)} %get-tuple-element.25, pred[2,1024,1024]{1,2,0:T(8,128)(4,1)S(1)} %get-tuple-element.29, f32[2,1024,2,2,128]{1,4,3,2,0:T(8,128)} %copy-done.6), kind=kOutput, calls=%fused_computation.24 | convolution fusion | flops 4378853376 | bytes 78708736 | tf_op jit(solution)/shard_map/rhgqk,rkhd->rhgqd/dot_general | solution.py:66
  591.0 0.3 fusion.61
  591.3 4.6 fusion.63
  595.9 21.7 %fusion.11 = f32[2,2,4,1024]{3,2,1,0:T(4,128)S(1)} fusion(f32[2,2,1024,1024,4]{3,2,4,1,0:T(8,128)} %get-tuple-element.42, f32[2,2,4,1024]{3,2,1,0:T(4,128)S(1)} %get-tuple-element.18, pred[2,1024,1024]{1,2,0:T(8,128)(4,1)S(1)} %copy-done.5), kind=kLoop, calls=%fused_computation.18 | loop fusion | flops 83869696 | bytes 69337088 | tf_op jit(solution)/shard_map/reduce_sum | solution.py:64
  617.5 42.6 %fusion.1 = f32[2,2,4,1024]{3,2,1,0:T(4,128)S(1)} fusion(f32[2,2,2048,1024,4]{3,2,4,1,0:T(8,128)} %get-tuple-element.40, f32[2,2,4,1024]{3,2,1,0:T(4,128)S(1)} %get-tuple-element.17, pred[2,1024,2048]{1,2,0:T(8,128)(4,1)} %fusion.30), kind=kLoop, calls=%fused_computation.3 | loop fusion | flops 167755776 | bytes 138543104 | tf_op jit(solution)/shard_map/reduce_sum | solution.py:64
  660.2 21.7 %fusion.13 = f32[2,2,4,1024]{3,2,1,0:T(4,128)S(1)} fusion(f32[2,2,1024,1024,4]{3,2,4,1,0:T(8,128)} %get-tuple-element.38, f32[2,2,4,1024]{3,2,1,0:T(4,128)S(1)} %get-tuple-element.16, pred[2,1024,1024]{1,2,0:T(8,128)(4,1)S(1)} %copy-done.4), kind=kLoop, calls=%fused_computation.20 | loop fusion | flops 83869696 | bytes 69337088 | tf_op jit(solution)/shard_map/reduce_sum | solution.py:64
  681.9 0.1 bitcast_add_fusion.5
  682.0 29.0 %fusion.17 = f32[2,2,4,1024,128]{3,4,2,1,0:T(8,128)} fusion(f32[2,2,1024,1024,4]{3,2,4,1,0:T(8,128)} %get-tuple-element.42, f32[2,2,4,1024]{3,2,1,0:T(4,128)S(1)} %get-tuple-element.18, pred[2,1024,1024]{1,2,0:T(8,128)(4,1)} %get-tuple-element.31, bf16[2,1024,2,2,128]{1,4,3,2,0:T(8,128)(2,1)} %collective-permute-done), kind=kOutput, calls=%fused_computation.23 | convolution fusion | flops 4378853376 | bytes 78708736 | tf_op jit(solution)/shard_map/rhgqk,rkhd->rhgqd/dot_general | solution.py:66
  711.0 50.0 %fusion.3 = f32[2,2,4,1024,128]{3,4,2,1,0:T(8,128)} fusion(f32[2,2,2048,1024,4]{3,2,4,1,0:T(8,128)} %get-tuple-element.40, f32[2,2,4,1024]{3,2,1,0:T(4,128)S(1)} %get-tuple-element.17, pred[2,1024,2048]{1,2,0:T(8,128)(4,1)} %fusion.30, bf16[2,2048,2,2,128]{1,4,3,2,0:T(8,128)(2,1)} %collective-permute-done.1), kind=kOutput, calls=%fused_computation.11 | convolution fusion | flops 8757706752 | bytes 148963328 | tf_op jit(solution)/shard_map/rhgqk,rkhd->rhgqd/dot_general | solution.py:66
  761.0 35.3 %fusion.32 = bf16[2,1024,2,4,128]{1,4,3,2,0:T(8,128)(2,1)} fusion(f32[2,2,4,1024,128]{3,4,2,1,0:T(8,128)} %fusion.63, f32[2,2,4,1024,128]{3,4,2,1,0:T(8,128)} %fusion.3, f32[2,2,4,1024,128]{3,4,2,1,0:T(8,128)} %fusion.17, f32[2,2,4,1024,128]{3,4,2,1,0:T(8,128)} %fusion.19, f32[2,1024,2,4]{1,3,2,0:T(4,128)S(1)} %get-tuple-element.11, ...), kind=kOutput, calls=%fused_computation.46 | convolution fusion | flops 4401922048 | bytes 108462080 | tf_op jit(solution)/shard_map/rhgqk,rkhd->rhgqd/dot_general | solution.py:66
  796.3 6.2 copy.59
  802.5 4.0 select_convert_fusion
  (45 shorter events, 0.1 us)
Async XLA Ops:
  7.2 204.0 %all-gather.3.cloned.1.call-start = ((), (), s32[]{:S(2)}) async-start(), calls=%async_computation.1 | async-start | bytes 25165824 | tf_op jit(solution)/shard_map/all_gather | solution.py:80
  33.1 11.7 %copy-start.13 = (s32[2,4]{1,0:T(2,128)S(1)}, s32[2,4]{1,0:T(2,128)}, u32[]{:S(2)}) copy-start(s32[2,4]{1,0:T(2,128)} %param.9) | copy-start | bytes 100
  33.1 12.0 %copy-start.16 = (s32[2]{0:T(128)S(1)}, s32[2]{0:T(128)}, u32[]{:S(2)}) copy-start(s32[2]{0:T(128)} %param.8) | copy-start | bytes 28
  45.4 346.0 %copy-start.9 = (pred[2,1024,4]{1,2,0:T(4,128)(4,1)}, pred[2,1024,4]{1,2,0:T(4,128)(4,1)S(1)}, u32[]{:S(2)}) copy-start(pred[2,1024,4]{1,2,0:T(4,128)(4,1)S(1)} %get-tuple-element.26) | copy-start | bytes 24580
  45.5 228.2 %copy-start.11 = (pred[2,1024]{1,0:T(4,128)(4,1)}, pred[2,1024]{1,0:T(4,128)(4,1)S(1)}, u32[]{:S(2)}) copy-start(pred[2,1024]{1,0:T(4,128)(4,1)S(1)} %get-tuple-element.32) | copy-start | bytes 6148
  211.1 13.5 %copy-start.7 = (f32[1024,64]{0,1:T(8,128)S(1)}, f32[1024,64]{0,1:T(8,128)}, u32[]{:S(2)}) copy-start(f32[1024,64]{0,1:T(8,128)} %get-tuple-element.28) | copy-start | bytes 786436
  224.3 15.2 %copy-start.6 = (f32[2,1024,2,2,128]{1,4,3,2,0:T(8,128)}, f32[2,1024,2,2,128]{1,4,3,2,0:T(8,128)S(1)}, u32[]{:S(2)}) copy-start(f32[2,1024,2,2,128]{1,4,3,2,0:T(8,128)S(1)} %fusion.26) | copy-start | bytes 12582916
  224.3 15.2 %slice-start = ((s8[8388608]{0:T(1024)(128)(4,1)}), s8[4194304]{0:T(1024)(128)(4,1)S(1)}, s32[]{:S(2)}) async-start(s8[8388608]{0:T(1024)(128)(4,1)} %bitcast.333), calls=%async_computation.2 | async-start | bytes 8388608
  224.6 2.3 copy-start.2
  224.6 14.9 %slice-start.1 = ((s8[8388608]{0:T(1024)(128)(4,1)}), s8[4194304]{0:T(1024)(128)(4,1)S(1)}, s32[]{:S(2)}) async-start(s8[8388608]{0:T(1024)(128)(4,1)} %bitcast.333), calls=%async_computation.3 | async-start | bytes 8388608
  228.5 167.1 %collective-permute-start = (bf16[2,1024,2,2,128]{1,4,3,2,0:T(8,128)(2,1)}, bf16[2,1024,2,2,128]{1,4,3,2,0:T(8,128)(2,1)}, u32[]{:S(2)}, u32[]{:S(2)}) collective-permute-start(bf16[2,1024,2,2,128]{1,4,3,2,0:T(8,128)(2,1)} %pad_maximum_fusion.1), channel_id=1, source_target_pairs={{0,2},{2,4},{4,6},{6,8},{8,10},{10,12},{12,14},{14,16},{16,18},{18... | collective-permute-start | bytes 6291464 | tf_op jit(solution)/shard_map/ppermute | solution.py:20
  233.5 195.9 %collective-permute-start.2 = (bf16[2,1024,2,2,128]{1,4,3,2,0:T(8,128)(2,1)}, bf16[2,1024,2,2,128]{1,4,3,2,0:T(8,128)(2,1)}, u32[]{:S(2)}, u32[]{:S(2)}) collective-permute-start(bf16[2,1024,2,2,128]{1,4,3,2,0:T(8,128)(2,1)} %pad_maximum_fusion.1), channel_id=1, source_target_pairs={{0,8},{2,10},{4,12},{6,14},{8,16},{10,18},{12,20},{14,22},{16,24},... | collective-permute-start | bytes 6291464 | tf_op jit(solution)/shard_map/ppermute | solution.py:20
  276.9 35.6 %all-to-all-start = ((bf16[2,2,1,1,1024,256]{4,5,0,3,2,1:T(8,128)(2,1)}), bf16[2,2,1,1,1024,256]{4,5,0,3,2,1:T(8,128)(2,1)}, u32[]{:S(2)}, u32[]{:S(2)}) async-start(bf16[2,2,1,1,1024,256]{4,5,0,3,2,1:T(8,128)(2,1)} %copy.60), calls=%async_computation | async-start | bytes 4194304 | tf_op jit(solution)/shard_map/all_to_all | solution.py:156
  286.6 2.0 copy-start
  391.4 38.0 %copy-start.14 = (bf16[2,4,2,2,128]{4,1,3,2,0:T(4,128)(2,1)}, bf16[2,4,2,2,128]{4,1,3,2,0:T(4,128)(2,1)S(1)}, u32[]{:S(2)}) copy-start(bf16[2,4,2,2,128]{4,1,3,2,0:T(4,128)(2,1)S(1)} %reduce_sum.64) | copy-start | bytes 24580
  391.4 12.4 %copy-start.1 = (bf16[2,1024,2,4,128]{4,1,3,2,0:T(8,128)(2,1)S(1)}, bf16[2,1024,2,4,128]{4,1,3,2,0:T(8,128)(2,1)}, u32[]{:S(2)}) copy-start(bf16[2,1024,2,4,128]{4,1,3,2,0:T(8,128)(2,1)} %copy-done) | copy-start | bytes 12582916
  399.2 92.5 %collective-permute-start.1 = (bf16[2,2048,2,2,128]{1,4,3,2,0:T(8,128)(2,1)}, bf16[2,2048,2,2,128]{1,4,3,2,0:T(8,128)(2,1)}, u32[]{:S(2)}, u32[]{:S(2)}) collective-permute-start(bf16[2,2048,2,2,128]{1,4,3,2,0:T(8,128)(2,1)} %maximum_maximum_fusion), channel_id=1, source_target_pairs={{0,4},{2,6},{4,8},{6,10},{8,12},{10,14},{12,16},{14,18},{16,20},{1... | collective-permute-start | bytes 12582920 | tf_op jit(solution)/shard_map/ppermute | solution.py:20
  403.7 25.6 %copy-start.3 = (pred[2,1024,1024]{1,2,0:T(8,128)(4,1)S(1)}, pred[2,1024,1024]{1,2,0:T(8,128)(4,1)}, u32[]{:S(2)}) copy-start(pred[2,1024,1024]{1,2,0:T(8,128)(4,1)} %get-tuple-element.30) | copy-start | bytes 6291460
  561.7 29.3 %copy-start.8 = (f32[2,2,4,1024,4]{3,4,2,1,0:T(4,128)S(1)}, f32[2,2,4,1024,4]{3,4,2,1,0:T(4,128)}, u32[]{:S(2)}) copy-start(f32[2,2,4,1024,4]{3,4,2,1,0:T(4,128)} %get-tuple-element.36) | copy-start | bytes 786436
  561.7 29.3 %copy-start.10 = (pred[2,1024,4]{1,2,0:T(4,128)(4,1)S(1)}, pred[2,1024,4]{1,2,0:T(4,128)(4,1)}, u32[]{:S(2)}) copy-start(pred[2,1024,4]{1,2,0:T(4,128)(4,1)} %copy-done.9) | copy-start | bytes 24580
  561.7 29.5 %copy-start.15 = (bf16[2,4,2,2,128]{4,1,3,2,0:T(4,128)(2,1)S(1)}, bf16[2,4,2,2,128]{4,1,3,2,0:T(4,128)(2,1)}, u32[]{:S(2)}) copy-start(bf16[2,4,2,2,128]{4,1,3,2,0:T(4,128)(2,1)} %copy-done.14) | copy-start | bytes 24580
  591.0 4.9 copy-start.5
  617.5 42.7 %copy-start.4 = (pred[2,1024,1024]{1,2,0:T(8,128)(4,1)S(1)}, pred[2,1024,1024]{1,2,0:T(8,128)(4,1)}, u32[]{:S(2)}) copy-start(pred[2,1024,1024]{1,2,0:T(8,128)(4,1)} %get-tuple-element.30) | copy-start | bytes 6291460
  796.3 6.2 copy-start.12
Sparse Core Ops, SparseCore 0:
  9.5 201.5 all-gather.2
